TPU v7x, 32 devices: a whole 2x2x4 slice. The times are simulated.
32 devices in a mesh: groups: 2 (over y), row: 4 (over z), col: 4 (over x, core).
Axes of the slice: x: 2, y: 2, z: 4, core: 2. Of those that a mesh axis runs over, the one named last changes fastest.
Arguments:
- prev_solution: float32 [16384, 1024], P(None, ('groups', 'row', 'col')), parts along dimension 1, may hold values from -6 to 6
- factor_panel: float32 [1024, 16384], P(None, ('row', 'col')), may hold values from -0.0625 to 0.0625
- right_side: float32 [1024, 1024], P('row', ('groups', 'col')), parts along dimension 1, may hold values from -6 to 6
- window_factor: float32 [1024, 1024], P('row'), may hold values from -2 to 2, as said below
Outputs:
- window_solution: float32 [1024, 1024], P('row', ('groups', 'col')), parts along dimension 1
There are 2 independent parts, one for each index of `groups`. A program takes and returns all parts, laid end to end along the dimension named above; an argument that names none is the same for every part. Nothing has to cross between parts.
Inputs may be any that keep to these rules, and one draw needn't show every extreme that they name: `window_factor`: lower triangular, with diagonal entries between 1 and 2.
All inputs are finite; a program needn't handle non-finite values.
Results may differ from a plain program's by a relative error of at most 0.0003.
Values sent between devices are 32-bit elements; how exact they have to be, the bound alone decides.
No kernel may reach another device: no remote copies, remote signals or barrier semaphores. Data moves between devices by JAX's collectives and lax.ppermute only.
A program may use at most 64 MiB of HBM per device.

v0:
```python
import jax
import jax.numpy as jnp
from jax import lax
from jax.sharding import PartitionSpec as P


def broadcast(value, axis, root):
    mine = lax.axis_index(axis) == root
    return lax.psum(jnp.where(mine, value, jnp.zeros_like(value)), axis)


def shards(prev_solution, factor_panel, right_side, window_factor):
    highest = lax.Precision.HIGHEST
    row_count = lax.axis_size("row")
    row_index = lax.axis_index("row")
    strip_rows = right_side.shape[0]
    by_rows = lax.all_to_all(prev_solution, ("row", "col"), split_axis=0, concat_axis=1, tiled=True)
    row_summed = lax.psum_scatter(
        jnp.dot(factor_panel, by_rows, precision=highest, preferred_element_type=jnp.float32),
        "row",
        scatter_dimension=0,
        tiled=True,
    )
    coupling = lax.psum_scatter(row_summed, "col", scatter_dimension=1, tiled=True)
    residual = right_side - coupling
    own_block = lax.dynamic_slice_in_dim(window_factor, row_index * strip_rows, strip_rows, 1)

    def sweep_step(strip_index, state_pair):
        pending, solved = state_pair
        candidate = jax.scipy.linalg.solve_triangular(own_block, pending, lower=True)
        arrived = broadcast(candidate, "row", strip_index)
        column_block = lax.dynamic_slice_in_dim(
            window_factor, strip_index * strip_rows, strip_rows, 1
        )
        update = jnp.dot(
            column_block, arrived, precision=highest, preferred_element_type=jnp.float32
        )
        pending = jnp.where(row_index > strip_index, pending - update, pending)
        solved = jnp.where(row_index == strip_index, arrived, solved)
        return (pending, solved)

    pending, solved = lax.fori_loop(0, row_count, sweep_step, (residual, jnp.zeros_like(residual)))
    return solved


def solution(mesh):
    in_specs = (
        P(None, ("groups", "row", "col")),
        P(None, ("row", "col")),
        P("row", ("groups", "col")),
        P("row", None),
    )
    out_specs = P("row", ("groups", "col"))
    return jax.shard_map(shards, mesh=mesh, in_specs=in_specs, out_specs=out_specs, check_vma=False)
```

profile of v0, /device:TPU:0, one launch (start us, length us, event | category | flops | bytes accessed | tf_op | source)
XLA Modules:
  0.0 303.0 jit_solution(4795972882912780716)
XLA Ops:
  6.5 1.7 copy.13
  8.3 54.7 %all_to_all.19 = f32[16,1024,32]{1,2,0:T(8,128)S(1)} all-to-all(f32[16,1024,32]{1,2,0:T(8,128)S(1)} %bitcast.42), channel_id=1, replica_groups=mesh['groups'=2,'row'=4,'col'=4] {'row','col'}, dimensions={0} | all-to-all | bytes 4194304 | tf_op jit(solution)/shard_map/all_to_all | solution.py:17
  63.0 8.1 %fusion.17 = f32[1024,512]{1,0:T(8,128)} fusion(f32[1024,1024]{1,0:T(8,128)S(1)} %copy-done, f32[1024,512]{0,1:T(8,128)S(1)} %bitcast.43), kind=kOutput, calls=%fused_computation.30 | convolution fusion | flops 6442450944 | bytes 8388608 | tf_op jit(solution)/shard_map/dot_general | solution.py:19
  71.2 44.4 %reduce-scatter.3.cloned.1.call-done = f32[256,512]{1,0:T(8,128)} async-done(((f32[1024,512]{1,0:T(8,128)}), f32[256,512]{1,0:T(8,128)}) %reduce-scatter.3.cloned.1.call-update) | async-done | bytes 524304 | tf_op jit(solution)/shard_map/reduce_scatter | solution.py:18
  115.8 4.3 %while.20 = (s32[]{:T(128)}, f32[256,256]{1,0:T(8,128)S(1)}, s32[2,2]{1,0:T(2,128)S(1)}, f32[2,128,128]{2,1,0:T(8,128)S(1)}, s32[]{:T(128)}) while((s32[]{:T(128)}, f32[256,256]{1,0:T(8,128)S(1)}, s32[2,2]{1,0:T(2,128)S(1)}, f32[2,128,128]{2,1,0:T(8,128)S(1)}, s32[]{:T(128)}) %tuple.62), condition=%wide.while_cond, body=%wide.while_body.sunk | while | flops 2 | bytes 131189 | solution.py:30
  115.8 0.7 fusion.33
  116.5 1.5 bitcast_dynamic-update-slice_fusion.2
  118.6 1.5 bitcast_dynamic-update-slice_fusion.2
  120.1 19.7 %custom-call.11 = f32[2,128,128]{1,2,0:T(8,128)S(1)} custom-call(f32[2,128,128]{2,1,0:T(8,128)S(1)} %get-tuple-element.195), custom_call_target="InvertDiagBlocksLowerTriangular" | custom-call | tf_op jit(solution)/shard_map/while/body/eval_jaxpr/jit(_solve_triangular)/triangular_solve | solution.py:30
  139.9 0.9 sub.13
  140.8 154.7 %while.21 = (s32[]{:T(128)}, f32[256,128]{1,0:T(8,128)S(1)}, f32[256,128]{1,0:T(8,128)S(1)}, s32[]{:T(128)}, f32[256,1024]{1,0:T(8,128)S(1)}, /*index=5*/f32[2,1...) while((s32[]{:T(128)}, f32[256,128]{1,0:T(8,128)S(1)}, ...), condition=%wide.region_4.5_spmd.clone, body=%wide.region_2.4_spmd.clone.sunk | while | flops 176472064 | bytes 2752807 | solution.py:42
  141.6 0.7 maximum_select_fusion.2
  142.3 35.6 %all-reduce.2.cloned.1.call-done = f32[256,128]{1,0:T(8,128)} async-done(((f32[256,128]{1,0:T(8,128)}), f32[256,128]{1,0:T(8,128)}) %all-reduce.2.cloned.1.call-update) | async-done | bytes 131088 | tf_op jit(solution)/shard_map/while/body/eval_jaxpr/psum | solution.py:9
  177.9 1.3 fusion.42
  179.2 0.9 select_select_fusion.2
  180.9 0.7 maximum_select_fusion.2
  181.6 34.7 %all-reduce.2.cloned.1.call-done = f32[256,128]{1,0:T(8,128)} async-done(((f32[256,128]{1,0:T(8,128)}), f32[256,128]{1,0:T(8,128)}) %all-reduce.2.cloned.1.call-update) | async-done | bytes 131088 | tf_op jit(solution)/shard_map/while/body/eval_jaxpr/psum | solution.py:9
  216.3 1.3 fusion.42
  218.4 0.7 maximum_select_fusion.2
  219.1 35.8 %all-reduce.2.cloned.1.call-done = f32[256,128]{1,0:T(8,128)} async-done(((f32[256,128]{1,0:T(8,128)}), f32[256,128]{1,0:T(8,128)}) %all-reduce.2.cloned.1.call-update) | async-done | bytes 131088 | tf_op jit(solution)/shard_map/while/body/eval_jaxpr/psum | solution.py:9
  254.9 1.3 fusion.42
  257.0 0.7 maximum_select_fusion.2
  257.7 36.4 %all-reduce.2.cloned.1.call-done = f32[256,128]{1,0:T(8,128)} async-done(((f32[256,128]{1,0:T(8,128)}), f32[256,128]{1,0:T(8,128)}) %all-reduce.2.cloned.1.call-update) | async-done | bytes 131088 | tf_op jit(solution)/shard_map/while/body/eval_jaxpr/psum | solution.py:9
  294.1 1.3 fusion.42
  (45 shorter events, 4.5 us)
Async XLA Ops:
  6.5 109.1 %reduce-scatter.3.cloned.1.call-start = ((), (), s32[]{:S(2)}) async-start(), calls=%async_computation.3 | async-start | bytes 2621440 | tf_op jit(solution)/shard_map/reduce_scatter | solution.py:18
  8.3 54.8 %copy-start = (f32[1024,1024]{1,0:T(8,128)S(1)}, f32[1024,1024]{1,0:T(8,128)}, u32[]{:S(2)}) copy-start(f32[1024,1024]{1,0:T(8,128)} %param.7) | copy-start | bytes 12582916
  71.1 44.6 %copy-start.2 = (f32[256,1024]{1,0:T(8,128)S(1)}, f32[256,1024]{1,0:T(8,128)}, u32[]{:S(2)}) copy-start(f32[256,1024]{1,0:T(8,128)} %param.9) | copy-start | bytes 3145732
  71.1 68.8 %copy-start.3 = (f32[256,128]{1,0:T(8,128)S(1)}, f32[256,128]{1,0:T(8,128)}, u32[]{:S(2)}) copy-start(f32[256,128]{1,0:T(8,128)} %param.8) | copy-start | bytes 393220
  71.1 68.8 %reduce-scatter.5.cloned.1.call-start = ((), (), s32[]{:S(2)}) async-start(), calls=%async_computation.4 | async-start | bytes 655360 | tf_op jit(solution)/shard_map/reduce_scatter | solution.py:24
  140.9 37.0 %all-reduce.2.cloned.1.call-start = ((), (), s32[]{:S(2)}) async-start(), calls=%async_computation.5 | async-start | bytes 262144 | tf_op jit(solution)/shard_map/while/body/eval_jaxpr/psum | solution.py:9
  180.2 36.1 %all-reduce.2.cloned.1.call-start = ((), (), s32[]{:S(2)}) async-start(), calls=%async_computation.5 | async-start | bytes 262144 | tf_op jit(solution)/shard_map/while/body/eval_jaxpr/psum | solution.py:9
  217.7 37.2 %all-reduce.2.cloned.1.call-start = ((), (), s32[]{:S(2)}) async-start(), calls=%async_computation.5 | async-start | bytes 262144 | tf_op jit(solution)/shard_map/while/body/eval_jaxpr/psum | solution.py:9
  256.3 37.9 %all-reduce.2.cloned.1.call-start = ((), (), s32[]{:S(2)}) async-start(), calls=%async_computation.5 | async-start | bytes 262144 | tf_op jit(solution)/shard_map/while/body/eval_jaxpr/psum | solution.py:9
  295.5 0.7 copy-start.1
Sparse Core Ops, SparseCore 0:
  71.2 44.3 reduce-scatter.2
  118.2 21.0 reduce-scatter.4
  144.0 33.8 all-reduce.1
  183.0 33.1 all-reduce.1
  220.5 34.3 all-reduce.1
  259.1 34.9 all-reduce.1
where the time goes:
time: 303 us
  waiting for transfers between devices  187 us (62%)
  blocking collectives  54.7 us (18%)
  other arithmetic  24.4 us (8%)
  matrix products  15.8 us (5%)
  between operations  13.5 us (4%)
  local copies, waits for them, and re-layouts  6.83 us (2%)
    psum x4, waiting for transfers between devices, broadcast(): return lax.psum(jnp.where(mine, value, jnp.zeros_like(value)), axis)  143 us
    all_to_all x1, blocking collectives, shards(): lax.all_to_all(prev_solution, ('row', 'col'), split_axis=0, concat_axis=1...  54.7 us
    reduce_scatter x1, waiting for transfers between devices, shards(): lax.psum_scatter(jnp.dot(factor_panel, by_rows, precision=highest, prefer...  44.4 us
    another operation x3, other arithmetic, sweep_step(): jax.scipy.linalg.solve_triangular(own_block, pending, lower=True)  19.7 us
    dot_general x1, matrix products, shards(): jnp.dot(factor_panel, by_rows, precision=highest, preferred_element_type=...  8.05 us
  transfers between devices with their start and end apart: 6, of which 5 were waited for; matrix products, arithmetic and copies ran while one was open for 8% of the time, Pallas kernels for 0%

commit v1 on v0

--- a/solution.py
+++ b/solution.py
@@ -4,9 +4,15 @@
 from jax.sharding import PartitionSpec as P
 
 
+def summed_here(x, name):
+    shards = lax.all_gather(x, name, axis=0, tiled=False)
+    summed = shards.sum(axis=0)
+    return summed
+
+
 def broadcast(value, axis, root):
     mine = lax.axis_index(axis) == root
-    return lax.psum(jnp.where(mine, value, jnp.zeros_like(value)), axis)
+    return summed_here(jnp.where(mine, value, jnp.zeros_like(value)), axis)
 
 
 def shards(prev_solution, factor_panel, right_side, window_factor):

time: 303 us -> 216 us (0.71)
  waiting for transfers between devices: 187 us -> 44.5 us
  blocking collectives: 54.7 us -> 117 us
  matrix products: 15.8 us -> 12.2 us
  other arithmetic: 24.4 us -> 20.9 us
    psum x4 -> x0, waiting for transfers between devices: 143 us -> none  [broadcast(): return lax.psum(jnp.where(mine, value, jnp.zeros_like(value)), axis)]
    all_gather x0 -> x4, blocking collectives: none -> 62.5 us  [summed_here(): shards = lax.all_gather(x, name, axis=0, tiled=False)]
    dot_general x4, matrix products: 5.28 us -> 1.68 us  [sweep_step(): jnp.dot(column_block, arrived, precision=highest, preferred_element_type=...]
  transfers between devices with their start and end apart: 6 -> 2, of which waited for: 5 -> 1; matrix products, arithmetic and copies ran while one was open for 8% -> 11% of each run, Pallas kernels for 0% -> 0%
where the time goes in v1:
time: 216 us; the launch traced here: 215 us
  blocking collectives  117 us (54%)
  waiting for transfers between devices  44.5 us (21%)
  other arithmetic  20.9 us (10%)
  between operations  13.5 us (6%)
  matrix products  12.2 us (6%)
  local copies, waits for them, and re-layouts  6.52 us (3%)
    all_gather x4, blocking collectives, summed_here(): shards = lax.all_gather(x, name, axis=0, tiled=False)  62.5 us
    all_to_all x1, blocking collectives, shards(): lax.all_to_all(prev_solution, ('row', 'col'), split_axis=0, concat_axis=1...  54.7 us
    reduce_scatter x1, waiting for transfers between devices, shards(): lax.psum_scatter(jnp.dot(factor_panel, by_rows, precision=highest, prefer...  44.4 us
    another operation x3, other arithmetic, sweep_step(): jax.scipy.linalg.solve_triangular(own_block, pending, lower=True)  19.7 us
    dot_general x1, matrix products, shards(): jnp.dot(factor_panel, by_rows, precision=highest, preferred_element_type=...  8.05 us
  transfers between devices with their start and end apart: 2, of which 1 were waited for; matrix products, arithmetic and copies ran while one was open for 11% of the time, Pallas kernels for 0%

profile of v1, /device:TPU:0, one launch (start us, length us, event | category | flops | bytes accessed | tf_op | source)
XLA Modules:
  0.0 215.4 jit_solution(9563377245543030978)
XLA Ops:
  6.5 1.7 copy.13
  8.3 54.7 %all_to_all.19 = f32[16,1024,32]{1,2,0:T(8,128)S(1)} all-to-all(f32[16,1024,32]{1,2,0:T(8,128)S(1)} %bitcast.48), channel_id=1, replica_groups=mesh['groups'=2,'row'=4,'col'=4] {'row','col'}, dimensions={0} | all-to-all | bytes 4194304 | tf_op jit(solution)/shard_map/all_to_all | solution.py:23
  63.0 8.1 %fusion.17 = f32[1024,512]{1,0:T(8,128)} fusion(f32[1024,1024]{1,0:T(8,128)S(1)} %copy-done, f32[1024,512]{0,1:T(8,128)S(1)} %bitcast.49), kind=kOutput, calls=%fused_computation.30 | convolution fusion | flops 6442450944 | bytes 8388608 | tf_op jit(solution)/shard_map/dot_general | solution.py:25
  71.1 44.4 %reduce-scatter.3.cloned.1.call-done = f32[256,512]{1,0:T(8,128)} async-done(((f32[1024,512]{1,0:T(8,128)}), f32[256,512]{1,0:T(8,128)}) %reduce-scatter.3.cloned.1.call-update) | async-done | bytes 524304 | tf_op jit(solution)/shard_map/reduce_scatter | solution.py:24
  115.8 4.0 %while.20 = (s32[]{:T(128)}, f32[256,256]{1,0:T(8,128)S(1)}, s32[2,2]{1,0:T(2,128)S(1)}, f32[2,128,128]{2,1,0:T(8,128)S(1)}, s32[]{:T(128)}) while((s32[]{:T(128)}, f32[256,256]{1,0:T(8,128)S(1)}, s32[2,2]{1,0:T(2,128)S(1)}, f32[2,128,128]{2,1,0:T(8,128)S(1)}, s32[]{:T(128)}) %tuple.62), condition=%wide.while_cond, body=%wide.while_body.sunk | while | flops 2 | bytes 131189 | solution.py:36
  115.8 0.6 fusion.33
  116.4 1.4 bitcast_dynamic-update-slice_fusion.2
  117.8 0.6 fusion.33
  118.4 1.4 bitcast_dynamic-update-slice_fusion.2
  119.8 19.7 %custom-call.11 = f32[2,128,128]{1,2,0:T(8,128)S(1)} custom-call(f32[2,128,128]{2,1,0:T(8,128)S(1)} %get-tuple-element.195), custom_call_target="InvertDiagBlocksLowerTriangular" | custom-call | tf_op jit(solution)/shard_map/while/body/eval_jaxpr/jit(_solve_triangular)/triangular_solve | solution.py:36
  139.6 0.9 sub.13
  140.5 67.3 %while.21 = (s32[]{:T(128)}, f32[256,128]{1,0:T(8,128)S(1)}, f32[256,128]{1,0:T(8,128)S(1)}, s32[]{:T(128)}, f32[256,1024]{1,0:T(8,128)S(1)}, /*index=5*/f32[2,1...) while((s32[]{:T(128)}, f32[256,128]{1,0:T(8,128)S(1)}, ...), condition=%wide.region_4.5_spmd.clone, body=%wide.region_2.4_spmd.clone.sunk | while | flops 176537600 | bytes 3277067 | solution.py:48
  141.2 15.4 %all_gather.15 = f32[4,256,128]{2,1,0:T(8,128)S(1)} all-gather(f32[1,256,128]{2,1,0:T(8,128)S(1)} %maximum_select_fusion.2), channel_id=1, replica_groups=mesh['groups'=2,'row'=4,'col'=4] {'row'}, dimensions={0}, use_global_device_ids=true | all-gather | bytes 655360 | tf_op jit(solution)/shard_map/while/body/eval_jaxpr/all_gather | solution.py:8
  156.7 0.4 fusion.42
  157.8 16.2 %all_gather.15 = f32[4,256,128]{2,1,0:T(8,128)S(1)} all-gather(f32[1,256,128]{2,1,0:T(8,128)S(1)} %maximum_select_fusion.2), channel_id=1, replica_groups=mesh['groups'=2,'row'=4,'col'=4] {'row'}, dimensions={0}, use_global_device_ids=true | all-gather | bytes 655360 | tf_op jit(solution)/shard_map/while/body/eval_jaxpr/all_gather | solution.py:8
  174.1 0.4 fusion.42
  175.3 16.2 %all_gather.15 = f32[4,256,128]{2,1,0:T(8,128)S(1)} all-gather(f32[1,256,128]{2,1,0:T(8,128)S(1)} %maximum_select_fusion.2), channel_id=1, replica_groups=mesh['groups'=2,'row'=4,'col'=4] {'row'}, dimensions={0}, use_global_device_ids=true | all-gather | bytes 655360 | tf_op jit(solution)/shard_map/while/body/eval_jaxpr/all_gather | solution.py:8
  191.5 0.4 fusion.42
  192.0 0.2 fusion.41
  192.2 0.2 convolution_subtract_fusion.3
  192.4 0.2 convolution_bitcast_fusion.2
  192.6 14.7 %all_gather.15 = f32[4,256,128]{2,1,0:T(8,128)S(1)} all-gather(f32[1,256,128]{2,1,0:T(8,128)S(1)} %maximum_select_fusion.2), channel_id=1, replica_groups=mesh['groups'=2,'row'=4,'col'=4] {'row'}, dimensions={0}, use_global_device_ids=true | all-gather | bytes 655360 | tf_op jit(solution)/shard_map/while/body/eval_jaxpr/all_gather | solution.py:8
  207.4 0.4 fusion.42
  207.9 0.6 copy-done.1
  (41 shorter events, 2.5 us)
Async XLA Ops:
  6.5 109.0 %reduce-scatter.3.cloned.1.call-start = ((), (), s32[]{:S(2)}) async-start(), calls=%async_computation.3 | async-start | bytes 2621440 | tf_op jit(solution)/shard_map/reduce_scatter | solution.py:24
  8.3 54.8 %copy-start = (f32[1024,1024]{1,0:T(8,128)S(1)}, f32[1024,1024]{1,0:T(8,128)}, u32[]{:S(2)}) copy-start(f32[1024,1024]{1,0:T(8,128)} %param.7) | copy-start | bytes 12582916
  71.1 44.6 %copy-start.2 = (f32[256,1024]{1,0:T(8,128)S(1)}, f32[256,1024]{1,0:T(8,128)}, u32[]{:S(2)}) copy-start(f32[256,1024]{1,0:T(8,128)} %param.9) | copy-start | bytes 3145732
  71.1 68.5 %copy-start.3 = (f32[256,128]{1,0:T(8,128)S(1)}, f32[256,128]{1,0:T(8,128)}, u32[]{:S(2)}) copy-start(f32[256,128]{1,0:T(8,128)} %param.8) | copy-start | bytes 393220
  71.1 68.5 %reduce-scatter.5.cloned.1.call-start = ((), (), s32[]{:S(2)}) async-start(), calls=%async_computation.4 | async-start | bytes 655360 | tf_op jit(solution)/shard_map/reduce_scatter | solution.py:30
  207.9 0.7 copy-start.1
Sparse Core Ops, SparseCore 0:
  71.2 44.3 reduce-scatter.2
  118.2 21.1 reduce-scatter.4
